TPU v7x, 128 devices: a whole 4x4x4 slice. The times are simulated.
128 devices in a mesh: depth: 4 (over x), sx: 4 (over y_hi, core), sy: 8 (over z, y_lo).
Axes of the slice: x: 4, y: 4 (y_hi: 2, y_lo: 2; y = y_hi * 2 + y_lo), z: 4, core: 2. Of those that a mesh axis runs over, the one named last changes fastest.
Arguments:
- density: float32 [128, 256, 1024], P('sx', 'sy', 'depth'), may hold values from -6 to 6
- kernel_taps: bfloat16 [2, 33], replicated, may hold values from 0.099609375 to 0.3984375
- tf_centre: float32 [8, 4], replicated, may hold values from -2 to 2
- tf_width: float32 [8, 4], replicated, may hold values from 0.4 to 1.5
- tf_color: float32 [8, 4, 3], replicated, may hold values from 0.05 to 1
- tf_opacity: float32 [8, 4], replicated, may hold values from 0.0005 to 0.004
- brick_tf: int32 [8, 16, 8], P('sx', 'sy', 'depth'), may hold values from 0 to 7
- view_order: int32 [8, 16], P('sx', 'sy'), may hold values from 0 to 1
Outputs:
- picture: float32 [4, 4, 4, 8, 256], P(None, 'sx', 'depth', None, 'sy')
Inputs may be any that keep to these rules, and one draw needn't show every extreme that they name: `view_order`: 0: the viewer of that column of bricks faces z = 0; 1: it faces z = 1023.
All inputs are finite; a program needn't handle non-finite values.
Results may differ from a plain program's by a relative error of at most 0.0003.
Values may be sent and summed in bfloat16 or wider, within the bound.
A program may use at most 64 MiB of HBM per device.

v0:
```python
import functools

import jax
import jax.numpy as jnp
from jax import lax
from jax.experimental import pallas as pl
from jax.experimental.pallas import tpu as pltpu
from jax.sharding import PartitionSpec as P

MESH = pl.DeviceIdType.MESH
LOG2E = 1.4426950408889634
CHUNKS = 4
SIDE = 16
CELLS = SIDE * SIDE
LANES = 128
SEGMENTS = 8


def band_tiles(taps_row, along_x, scale):
    shifted = pltpu.roll(
        jnp.broadcast_to(taps_row, (LANES, LANES)), 0, axis=1, stride=1, stride_axis=0
    ).astype(jnp.bfloat16)

    def part(index):
        return index // SIDE if along_x else index % SIDE

    def other(index):
        return index % SIDE if along_x else index // SIDE

    row = lax.broadcasted_iota(jnp.int32, (3 * CELLS, LANES), 0)
    tap = lax.broadcasted_iota(jnp.int32, (3 * CELLS, LANES), 1)
    left = (tap == part(row % CELLS) + SIDE * (row // CELLS)).astype(jnp.float32)
    first = lax.dot_general(
        left.astype(jnp.bfloat16),
        shifted,
        (((1,), (1,)), ((), ())),
        preferred_element_type=jnp.float32,
    ).astype(jnp.bfloat16)
    target = lax.broadcasted_iota(jnp.int32, (LANES, CELLS), 0)
    column = lax.broadcasted_iota(jnp.int32, (LANES, CELLS), 1)
    right = (target == part(column)).astype(jnp.float32).astype(jnp.bfloat16)
    full = jnp.dot(first, right, preferred_element_type=jnp.float32)
    row = lax.broadcasted_iota(jnp.int32, (3 * CELLS, CELLS), 0)
    column = lax.broadcasted_iota(jnp.int32, (3 * CELLS, CELLS), 1)
    keep = other(row % CELLS) == other(column)
    return jnp.where(keep, full * scale, 0.0).astype(jnp.bfloat16)


def kernel(
    counts,
    density_hbm,
    taps_ref,
    centre_ref,
    width_ref,
    color_ref,
    opacity_ref,
    brick_ref,
    order_ref,
    out_ref,
    density,
    turned,
    coarse,
    x_halo,
    across,
    y_halo,
    weighted,
    band_x,
    band_y,
    taps_wide,
    running,
    sums,
    share,
    colours,
    clear,
    colours_in,
    clear_in,
    load_sem,
    x_send,
    x_recv,
    y_send,
    y_recv,
    t_send,
    t_recv,
    c_send,
    c_recv,
):
    n_depth, n_sx, n_sy = counts
    depth, sx, sy = lax.axis_index("depth"), lax.axis_index("sx"), lax.axis_index("sy")
    rows_z = turned.shape[1]
    steps = rows_z // SEGMENTS
    chunk = rows_z // CHUNKS
    steps_chunk = steps // CHUNKS
    has = {
        ("sx", 0): sx > 0,
        ("sx", 1): sx < n_sx - 1,
        ("sy", 0): sy > 0,
        ("sy", 1): sy < n_sy - 1,
    }
    near = {
        ("sx", 0): {"sx": jnp.maximum(sx - 1, 0)},
        ("sx", 1): {"sx": jnp.minimum(sx + 1, n_sx - 1)},
        ("sy", 0): {"sy": jnp.maximum(sy - 1, 0)},
        ("sy", 1): {"sy": jnp.minimum(sy + 1, n_sy - 1)},
    }

    loads = []
    for half in range(2):
        copy = pltpu.make_async_copy(
            density_hbm.at[pl.ds(half * SIDE, SIDE)],
            density.at[pl.ds(half * SIDE, SIDE)],
            load_sem.at[half],
        )
        copy.start()
        loads.append(copy)

    barrier = pltpu.get_barrier_semaphore()
    for key, there in has.items():

        @pl.when(there)
        def _(key=key):
            pl.semaphore_signal(barrier, inc=1, device_id=near[key], device_id_type=MESH)

    for step in range(1, n_depth):
        pl.semaphore_signal(
            barrier,
            inc=1,
            device_id={"depth": lax.rem(depth + step, n_depth)},
            device_id_type=MESH,
        )

    for axis, halo in (("sx", x_halo), ("sy", y_halo)):
        for side in range(2):

            @pl.when(jnp.logical_not(has[axis, side]))
            def _(halo=halo, side=side):
                halo[side] = jnp.zeros(halo.shape[1:], halo.dtype)

    for half in range(2):
        loads[half].wait()
        for y_half in range(2):
            tile = half * 2 + y_half
            for part in range(2):
                x_at = half * SIDE + part * (SIDE // 2)
                piece = density[x_at : x_at + SIDE // 2, y_half * SIDE : (y_half + 1) * SIDE, :]
                turned[tile * 2 + part] = piece.reshape(LANES, rows_z).T

    @pl.loop(0, steps // 2)
    def _(pair):
        for block in range(8):
            tile, part = block // 2, block % 2
            half, y_half = tile // 2, tile % 2
            both = jnp.concatenate(
                [
                    turned[block, pl.ds(pair * 2, SEGMENTS, stride=steps), :],
                    turned[block, pl.ds(pair * 2 + 1, SEGMENTS, stride=steps), :],
                ],
                axis=0,
            )
            lane = y_half * CELLS + part * LANES
            coarse[half, pl.ds(pl.multiple_of(pair * 16, 16), 16), lane : lane + LANES] = (
                both.astype(jnp.bfloat16)
            )

    waits = n_depth - 1
    for there in has.values():
        waits = waits + there.astype(jnp.int32)
    pl.semaphore_wait(barrier, waits)

    def halo_copy(axis, side, at):
        source, halo, send, recv = (
            (coarse, x_halo, x_send, x_recv)
            if axis == "sx"
            else (across, y_halo, y_send, y_recv)
        )
        rows = pl.ds(at * chunk, chunk)
        return pltpu.make_async_remote_copy(
            src_ref=source.at[side, rows],
            dst_ref=halo.at[1 - side, rows],
            send_sem=send.at[side, at],
            recv_sem=recv.at[1 - side, at],
            device_id=near[axis, side],
            device_id_type=MESH,
        )

    def halo_arrival(axis, side, at):
        halo, send, recv = (
            (x_halo, x_send, x_recv) if axis == "sx" else (y_halo, y_send, y_recv)
        )
        rows = pl.ds(at * chunk, chunk)
        return pltpu.make_async_remote_copy(
            src_ref=halo.at[side, rows],
            dst_ref=halo.at[side, rows],
            send_sem=send.at[side, at],
            recv_sem=recv.at[side, at],
            device_id=near[axis, side],
            device_id_type=MESH,
        )

    for at in range(CHUNKS):
        for side in range(2):

            @pl.when(has["sx", side])
            def _(side=side, at=at):
                halo_copy("sx", side, at).start()

    taps_wide[...] = jnp.zeros(taps_wide.shape, taps_wide.dtype)
    taps_wide[0:2, 0 : taps_ref.shape[1]] = taps_ref[...].astype(jnp.float32)
    band_x[...] = band_tiles(taps_wide[0:1, :], True, 1.0)
    band_y[...] = band_tiles(taps_wide[1:2, :], False, 0.5)

    first_brick = lax.broadcasted_iota(jnp.int32, (SEGMENTS, LANES), 0) < SEGMENTS // 2

    def table(ref, tile, *rest):
        half, y_half = tile // 2, lax.rem(tile, 2)
        return jnp.where(
            first_brick,
            ref[(brick_ref[half, y_half, 0],) + rest],
            ref[(brick_ref[half, y_half, 1],) + rest],
        )

    def reversed_tile(tile):
        return order_ref[tile // 2, lax.rem(tile, 2)] == 1

    @pl.loop(0, 4)
    def _(tile):
        sign = jnp.where(reversed_tile(tile), LOG2E, -LOG2E).astype(jnp.float32)
        centre = [table(centre_ref, tile, bump) for bump in range(4)]
        width = [table(width_ref, tile, bump) for bump in range(4)]
        narrow = [-LOG2E / (each * each) for each in width]
        thick = [table(opacity_ref, tile, bump) * sign for bump in range(4)]

        def body(step, carry):
            after = []
            for part in range(2):
                block = tile * 2 + part
                cells = turned[block, pl.ds(step, SEGMENTS, stride=steps), :]
                bumps = []
                optical = None
                for bump in range(4):
                    away = cells - centre[bump]
                    value = jnp.exp2(away * away * narrow[bump])
                    bumps.append(value)
                    term = thick[bump] * value
                    optical = term if optical is None else optical + term
                nearer = carry[part] * jnp.exp2(optical)
                weight = carry[part] - nearer
                rows = pl.ds(pl.multiple_of(step * SEGMENTS, SEGMENTS), SEGMENTS)
                for bump in range(4):
                    weighted[bump, block, rows, :] = weight * bumps[bump]
                after.append(nearer)
            return tuple(after)

        ones = jnp.ones((SEGMENTS, LANES), jnp.float32)
        ends = lax.fori_loop(0, steps, body, (ones, ones), unroll=4)
        for part in range(2):
            running[tile * 2 + part] = ends[part]

    def blur(at, source, halo, band):
        rows = slice(at * chunk, (at + 1) * chunk)
        lines = []
        for half in range(2):
            for other in range(2):
                lanes = slice(other * CELLS, (other + 1) * CELLS)
                before = halo[0, rows, lanes] if half == 0 else source[0, rows, lanes]
                behind = halo[1, rows, lanes] if half == 1 else source[1, rows, lanes]
                lines.append(
                    jnp.concatenate([before, source[half, rows, lanes], behind], axis=1)
                )
        return jnp.dot(
            jnp.concatenate(lines, axis=0), band[...], preferred_element_type=jnp.float32
        )

    for at in range(CHUNKS):
        for side in range(2):

            @pl.when(has["sx", side])
            def _(side=side, at=at):
                halo_arrival("sx", side, at).wait_recv()

        result = blur(at, coarse, x_halo, band_x).astype(jnp.bfloat16)
        for half in range(2):
            for y_half in range(2):
                place = half * 2 + y_half
                across[
                    y_half, at * chunk : (at + 1) * chunk, half * CELLS : (half + 1) * CELLS
                ] = result[place * chunk : (place + 1) * chunk]
        for side in range(2):

            @pl.when(has["sy", side])
            def _(side=side, at=at):
                halo_copy("sy", side, at).start()

    sublane = lax.broadcasted_iota(jnp.int32, (SEGMENTS, LANES), 0)
    for block in range(8):
        tile, part = block // 2, block % 2
        half, y_half = tile // 2, tile % 2
        back = order_ref[half, y_half] == 1
        end = running[block]
        through = jnp.where(back, 1.0 / end, end)
        forth, aback = through, through
        for shift in (1, 2, 4):
            forth = forth * jnp.where(sublane >= shift, pltpu.roll(forth, shift, axis=0), 1.0)
            aback = aback * jnp.where(
                sublane < SEGMENTS - shift, pltpu.roll(aback, SEGMENTS - shift, axis=0), 1.0
            )
        in_front = jnp.where(
            back,
            jnp.where(sublane < SEGMENTS - 1, pltpu.roll(aback, SEGMENTS - 1, axis=0), 1.0),
            jnp.where(sublane >= 1, pltpu.roll(forth, 1, axis=0), 1.0),
        )
        share[block] = in_front * jnp.where(back, -0.5 * through, 0.5)
        owner = half * 2 + part
        for channel in range(4):
            clear[owner, channel * 2 + y_half : channel * 2 + y_half + 1, :] = aback[0:1, :]

    def depth_copy(step, source, target, send, recv):
        peer = lax.rem(depth + step, n_depth)
        return pltpu.make_async_remote_copy(
            src_ref=source.at[peer],
            dst_ref=target.at[depth],
            send_sem=send.at[step - 1],
            recv_sem=recv.at[step - 1],
            device_id={"depth": peer},
            device_id_type=MESH,
        )

    clear_copies = [
        depth_copy(step, clear, clear_in, t_send, t_recv) for step in range(1, n_depth)
    ]
    for copy in clear_copies:
        copy.start()
    clear_in[depth] = clear[depth]

    for at in range(CHUNKS):
        for side in range(2):

            @pl.when(has["sy", side])
            def _(side=side, at=at):
                halo_arrival("sy", side, at).wait_recv()

        shade = 1.0 - jnp.tanh(blur(at, across, y_halo, band_y))
        for y_half in range(2):
            for half in range(2):
                tile = half * 2 + y_half
                place = y_half * 2 + half
                for part in range(2):
                    block = tile * 2 + part
                    for bump in range(4):
                        total = None
                        for step in range(steps_chunk):
                            row = step * SEGMENTS
                            term = (
                                weighted[
                                    bump,
                                    block,
                                    at * chunk + row : at * chunk + row + SEGMENTS,
                                    :,
                                ]
                                * shade[
                                    place * chunk + row : place * chunk + row + SEGMENTS,
                                    part * LANES : (part + 1) * LANES,
                                ]
                            )
                            total = term if total is None else total + term
                        if at == 0:
                            sums[bump, block] = total
                        else:
                            sums[bump, block] += total

    for block in range(8):
        tile, part = block // 2, block % 2
        half, y_half = tile // 2, tile % 2
        owner = half * 2 + part
        for channel in range(3):
            mixed = None
            for bump in range(4):
                term = table(color_ref, tile, bump, channel) * sums[bump, block]
                mixed = term if mixed is None else mixed + term
            row = channel * 2 + y_half
            colours[owner, row : row + 1, :] = jnp.sum(mixed * share[block], axis=0, keepdims=True)
        colours[owner, 6 + y_half : 7 + y_half, :] = jnp.zeros((1, LANES), jnp.float32)

    colour_copies = [
        depth_copy(step, colours, colours_in, c_send, c_recv) for step in range(1, n_depth)
    ]
    for copy in colour_copies:
        copy.start()
    colours_in[depth] = colours[depth]

    for copy in clear_copies:
        copy.wait()
    own_half = depth // 2
    odd = lax.rem(sublane, 2) == 1
    back_rows = (
        jnp.where(odd, order_ref[own_half, 1], order_ref[own_half, 0]) == 1
    )
    ones = jnp.ones((SEGMENTS, LANES), jnp.float32)
    forth, aback = [ones], [ones]
    for at in range(n_depth):
        forth.append(forth[-1] * clear_in[at])
        aback.append(aback[-1] * clear_in[n_depth - 1 - at])
    for copy in colour_copies:
        copy.wait()
    image = None
    for at in range(n_depth):
        in_front = jnp.where(back_rows, aback[n_depth - 1 - at], forth[at])
        term = in_front * colours_in[at]
        image = term if image is None else image + term
    out_ref[...] = jnp.where(sublane >= 6, 1.0 - forth[n_depth], image)

    for axis in ("sx", "sy"):
        for side in range(2):
            for at in range(CHUNKS):

                @pl.when(has[axis, side])
                def _(axis=axis, side=side, at=at):
                    halo_copy(axis, side, at).wait_send()


def per_device(
    counts, density, kernel_taps, tf_centre, tf_width, tf_color, tf_opacity, brick_tf, view_order
):
    rows_x, rows_y, rows_z = density.shape
    n_depth = counts[0]
    f32, bf16 = jnp.float32, jnp.bfloat16
    smem = pl.BlockSpec(memory_space=pltpu.SMEM)
    vmem = pl.BlockSpec(memory_space=pltpu.VMEM)
    picture = pl.pallas_call(
        functools.partial(kernel, counts),
        out_shape=jax.ShapeDtypeStruct((8, LANES), f32),
        in_specs=[pl.BlockSpec(memory_space=pl.ANY), vmem] + [smem] * 6,
        out_specs=vmem,
        scratch_shapes=[
            pltpu.VMEM((rows_x, rows_y, rows_z), f32),
            pltpu.VMEM((8, rows_z, LANES), f32),
            pltpu.VMEM((2, rows_z, 2 * CELLS), bf16),
            pltpu.VMEM((2, rows_z, 2 * CELLS), bf16),
            pltpu.VMEM((2, rows_z, 2 * CELLS), bf16),
            pltpu.VMEM((2, rows_z, 2 * CELLS), bf16),
            pltpu.VMEM((4, 8, rows_z, LANES), f32),
            pltpu.VMEM((3 * CELLS, CELLS), bf16),
            pltpu.VMEM((3 * CELLS, CELLS), bf16),
            pltpu.VMEM((8, LANES), f32),
            pltpu.VMEM((8, SEGMENTS, LANES), f32),
            pltpu.VMEM((4, 8, SEGMENTS, LANES), f32),
            pltpu.VMEM((8, SEGMENTS, LANES), f32),
            pltpu.VMEM((n_depth, 8, LANES), f32),
            pltpu.VMEM((n_depth, 8, LANES), f32),
            pltpu.VMEM((n_depth, 8, LANES), f32),
            pltpu.VMEM((n_depth, 8, LANES), f32),
            pltpu.SemaphoreType.DMA((2,)),
            pltpu.SemaphoreType.DMA((2, CHUNKS)),
            pltpu.SemaphoreType.DMA((2, CHUNKS)),
            pltpu.SemaphoreType.DMA((2, CHUNKS)),
            pltpu.SemaphoreType.DMA((2, CHUNKS)),
            pltpu.SemaphoreType.DMA((n_depth - 1,)),
            pltpu.SemaphoreType.DMA((n_depth - 1,)),
            pltpu.SemaphoreType.DMA((n_depth - 1,)),
            pltpu.SemaphoreType.DMA((n_depth - 1,)),
        ],
        compiler_params=pltpu.CompilerParams(collective_id=0, has_side_effects=True),
    )(density, kernel_taps, tf_centre, tf_width, tf_color, tf_opacity, brick_tf, view_order)
    picture = picture.reshape(4, 2, rows_x // n_depth, SIDE).transpose(0, 2, 1, 3)
    return picture.reshape(4, 1, 1, rows_x // n_depth, rows_y)


def solution(mesh):
    counts = tuple(mesh.shape[axis] for axis in ("depth", "sx", "sy"))
    return jax.shard_map(
        functools.partial(per_device, counts),
        mesh=mesh,
        in_specs=(
            P("sx", "sy", "depth"),
            P(),
            P(),
            P(),
            P(),
            P(),
            P("sx", "sy", "depth"),
            P("sx", "sy"),
        ),
        out_specs=P(None, "sx", "depth", None, "sy"),
        check_vma=False,
    )
```

profile of v0, /device:TPU:24, one launch (start us, length us, event | category | flops | bytes accessed | tf_op | source)
XLA Modules:
  0.0 31.4 jit_solution(14425397443540701419)
XLA Ops:
  0.0 0.0 copy-start.1
  0.0 0.0 copy-start.2
  0.0 1.4 %copy.9.centre_ref = f32[8,4]{1,0:T(8,128)} copy(f32[8,4]{0,1:T(4,128)} %param.10) | data formatting | bytes 256 | tf_op args[2]
  1.4 0.0 copy-done.1
  1.4 0.0 copy-start
  1.4 0.7 %copy.10.width_ref = f32[8,4]{1,0:T(8,128)} copy(f32[8,4]{0,1:T(4,128)S(1)} %copy-done.1) | data formatting | bytes 256 | tf_op args[3]
  2.1 0.0 copy-done.2
  2.1 0.7 %copy.12.opacity_ref = f32[8,4]{1,0:T(8,128)} copy(f32[8,4]{0,1:T(4,128)S(1)} %copy-done.2) | data formatting | bytes 256 | tf_op args[5]
  2.7 0.0 copy-done
  2.7 0.7 %copy.11.color_ref = f32[8,4,3]{2,1,0:T(4,128)} copy(f32[8,4,3]{0,1,2:T(4,128)S(1)} %copy-done) | data formatting | bytes 768 | tf_op args[4]
  3.4 26.5 %shard_map.82 = f32[8,128]{1,0:T(8,128)} custom-call(f32[32,32,256]{2,1,0:T(8,128)} %density_hbm.1, bf16[2,33]{1,0:T(2,128)(2,1)} %taps_ref.1, f32[8,4]{1,0:T(8,128)} %copy.9.centre_ref, f32[8,4]{1,0:T(8,128)} %copy.10.width_ref, f32[8,4,3]{2,1,0:T(4,128)} %copy.11.color_ref, f32[8,4]{1,0:T(8,128)} %copy.12.opacity_ref, s32[2,2,2]{2,1,0:T(2,128)} %brick_ref.1, ...), custom_call_target="tpu_custom_call" | custom-call | tf_op jit(solution)/shard_map/pallas_call | solution.py:428
  30.0 0.8 %reshape.6 = f32[4,2,8,16]{3,2,1,0:T(8,128)S(1)} reshape(f32[8,128]{1,0:T(8,128)} %shard_map.82) | data formatting | bytes 8192 | tf_op jit(solution)/shard_map/reshape | solution.py:463
  30.7 0.7 %reshape.7 = f32[4,1,1,8,32]{4,3,2,1,0:T(8,128)} reshape(f32[4,8,2,16]{3,2,1,0:T(2,128)S(1)} %copy.13) | data formatting | bytes 8192 | tf_op jit(solution)/shard_map/reshape | solution.py:464
  (1 shorter events, 0.0 us)
Async XLA Ops:
  0.0 1.4 %copy-start.1 = (f32[8,4]{0,1:T(4,128)S(1)}, f32[8,4]{0,1:T(4,128)}, u32[]{:S(2)}) copy-start(f32[8,4]{0,1:T(4,128)} %param.11) | copy-start | bytes 388
  0.0 2.1 %copy-start.2 = (f32[8,4]{0,1:T(4,128)S(1)}, f32[8,4]{0,1:T(4,128)}, u32[]{:S(2)}) copy-start(f32[8,4]{0,1:T(4,128)} %param.13) | copy-start | bytes 388
  1.4 1.3 %copy-start = (f32[8,4,3]{0,1,2:T(4,128)S(1)}, f32[8,4,3]{0,1,2:T(4,128)}, u32[]{:S(2)}) copy-start(f32[8,4,3]{0,1,2:T(4,128)} %param.12) | copy-start | bytes 1156
where the time goes:
time: 31.7 us; the launch traced here: 31.4 us
  Pallas kernels  26.5 us (84%)
  local copies, waits for them, and re-layouts  4.89 us (15%)
    pallas_call x1, Pallas kernels, per_device(): pl.pallas_call(functools.partial(kernel, counts), out_shape=jax.ShapeDtyp...  26.5 us
    unnamed x10, local copies, waits for them, and re-layouts  3.43 us
    reshape x1, local copies, waits for them, and re-layouts, per_device(): picture.reshape(4, 2, rows_x // n_depth, SIDE).transpose(0, 2, 1, 3)  0.76 us
    reshape x1, local copies, waits for them, and re-layouts, per_device(): return picture.reshape(4, 1, 1, rows_x // n_depth, rows_y)  0.69 us

commit v1 on v0

--- a/solution.py
+++ b/solution.py
@@ -214,8 +214,8 @@
         half, y_half = tile // 2, lax.rem(tile, 2)
         return jnp.where(
             first_brick,
-            ref[(brick_ref[half, y_half, 0],) + rest],
-            ref[(brick_ref[half, y_half, 1],) + rest],
+            ref[rest + (brick_ref[half, y_half, 0],)],
+            ref[rest + (brick_ref[half, y_half, 1],)],
         )
 
     def reversed_tile(tile):
@@ -374,7 +374,7 @@
         for channel in range(3):
             mixed = None
             for bump in range(4):
-                term = table(color_ref, tile, bump, channel) * sums[bump, block]
+                term = table(color_ref, tile, channel, bump) * sums[bump, block]
                 mixed = term if mixed is None else mixed + term
             row = channel * 2 + y_half
             colours[owner, row : row + 1, :] = jnp.sum(mixed * share[block], axis=0, keepdims=True)
@@ -406,7 +406,19 @@
         in_front = jnp.where(back_rows, aback[n_depth - 1 - at], forth[at])
         term = in_front * colours_in[at]
         image = term if image is None else image + term
-    out_ref[...] = jnp.where(sublane >= 6, 1.0 - forth[n_depth], image)
+    image = jnp.where(sublane >= 6, 1.0 - forth[n_depth], image)
+    low = lax.broadcasted_iota(jnp.int32, (SEGMENTS, LANES), 1) < SIDE
+    for channel in range(4):
+        halves = []
+        for y_half in range(2):
+            row = channel * 2 + y_half
+            line = jnp.broadcast_to(image[row : row + 1, :], (SEGMENTS, LANES))
+            for bit in (4, 2, 1):
+                line = jnp.where(
+                    (sublane & bit) != 0, pltpu.roll(line, LANES - SIDE * bit, axis=1), line
+                )
+            halves.append(pltpu.roll(line, SIDE, axis=1) if y_half else line)
+        out_ref[channel] = jnp.where(low, halves[0], halves[1])[:, : 2 * SIDE]
 
     for axis in ("sx", "sy"):
         for side in range(2):
@@ -427,7 +439,7 @@
     vmem = pl.BlockSpec(memory_space=pltpu.VMEM)
     picture = pl.pallas_call(
         functools.partial(kernel, counts),
-        out_shape=jax.ShapeDtypeStruct((8, LANES), f32),
+        out_shape=jax.ShapeDtypeStruct((4, rows_x // n_depth, rows_y), f32),
         in_specs=[pl.BlockSpec(memory_space=pl.ANY), vmem] + [smem] * 6,
         out_specs=vmem,
         scratch_shapes=[
@@ -459,8 +471,16 @@
             pltpu.SemaphoreType.DMA((n_depth - 1,)),
         ],
         compiler_params=pltpu.CompilerParams(collective_id=0, has_side_effects=True),
-    )(density, kernel_taps, tf_centre, tf_width, tf_color, tf_opacity, brick_tf, view_order)
-    picture = picture.reshape(4, 2, rows_x // n_depth, SIDE).transpose(0, 2, 1, 3)
+    )(
+        density,
+        kernel_taps,
+        tf_centre.T,
+        tf_width.T,
+        tf_color.transpose(2, 1, 0),
+        tf_opacity.T,
+        brick_tf,
+        view_order,
+    )
     return picture.reshape(4, 1, 1, rows_x // n_depth, rows_y)
 
 

time: 31.7 us -> 28.1 us (0.89)
  local copies, waits for them, and re-layouts: 4.89 us -> 1.32 us
    unnamed x10 -> x1, local copies, waits for them, and re-layouts: 3.43 us -> 1.32 us
    reshape x2 -> x0, local copies, waits for them, and re-layouts: 1.45 us -> none  [the longest x1 0.76 us: per_device(): picture.reshape(4, 2, rows_x // n_depth, SIDE).transpose(0, 2, 1, 3)]
where the time goes in v1:
time: 28.1 us; the launch traced here: 27.9 us
  Pallas kernels  26.5 us (94%)
  local copies, waits for them, and re-layouts  1.32 us (5%)
    pallas_call x1, Pallas kernels, per_device(): pl.pallas_call(functools.partial(kernel, counts), out_shape=jax.ShapeDtyp...  26.5 us
    unnamed x1, local copies, waits for them, and re-layouts  1.32 us

profile of v1, /device:TPU:24, one launch (start us, length us, event | category | flops | bytes accessed | tf_op | source)
XLA Modules:
  0.0 27.9 jit_solution(3347238793087292041)
XLA Ops:
  0.0 26.5 %shard_map.82 = f32[4,8,32]{2,1,0:T(8,128)} custom-call(f32[32,32,256]{2,1,0:T(8,128)} %density_hbm.1, bf16[2,33]{1,0:T(2,128)(2,1)} %taps_ref.1, f32[4,8]{1,0:T(4,128)} %bitcast.9, f32[4,8]{1,0:T(4,128)} %bitcast.10, f32[3,4,8]{2,1,0:T(4,128)} %bitcast.8, f32[4,8]{1,0:T(4,128)} %bitcast.11, s32[2,2,2]{2,1,0:T(2,128)} %brick_ref.1, s32[2,2]{1,0:T(2,128)} %order_ref.1), custom_call_target="tpu_custom_call" | custom-call | tf_op jit(solution)/shard_map/pallas_call | solution.py:440
  26.5 1.3 %copy.11 = f32[4,1,1,8,32]{4,3,2,1,0:T(8,128)} copy(f32[4,1,1,8,32]{4,3,2,1,0:T(8,128)} %bitcast.7) | data formatting | bytes 8192

commit v2 on v1

--- a/solution.py
+++ b/solution.py
@@ -103,6 +103,12 @@
         ("sy", 1): {"sy": jnp.minimum(sy + 1, n_sy - 1)},
     }
 
+    near_half = 1 - lax.rem(sx, 2)
+    far_half = lax.rem(sx, 2)
+    has_far = jnp.logical_and(sx > 0, sx < n_sx - 1)
+    near_core = {"sx": sx + 2 * near_half - 1}
+    far_core = {"sx": jnp.clip(sx + 2 * far_half - 1, 0, n_sx - 1)}
+
     loads = []
     for half in range(2):
         copy = pltpu.make_async_copy(
@@ -144,64 +150,79 @@
                 piece = density[x_at : x_at + SIDE // 2, y_half * SIDE : (y_half + 1) * SIDE, :]
                 turned[tile * 2 + part] = piece.reshape(LANES, rows_z).T
 
-    @pl.loop(0, steps // 2)
-    def _(pair):
-        for block in range(8):
-            tile, part = block // 2, block % 2
-            half, y_half = tile // 2, tile % 2
-            both = jnp.concatenate(
-                [
-                    turned[block, pl.ds(pair * 2, SEGMENTS, stride=steps), :],
-                    turned[block, pl.ds(pair * 2 + 1, SEGMENTS, stride=steps), :],
-                ],
-                axis=0,
-            )
-            lane = y_half * CELLS + part * LANES
-            coarse[half, pl.ds(pl.multiple_of(pair * 16, 16), 16), lane : lane + LANES] = (
-                both.astype(jnp.bfloat16)
-            )
-
     waits = n_depth - 1
     for there in has.values():
         waits = waits + there.astype(jnp.int32)
     pl.semaphore_wait(barrier, waits)
 
-    def halo_copy(axis, side, at):
-        source, halo, send, recv = (
-            (coarse, x_halo, x_send, x_recv)
-            if axis == "sx"
-            else (across, y_halo, y_send, y_recv)
-        )
+    def x_copy(side, core, at):
         rows = pl.ds(at * chunk, chunk)
         return pltpu.make_async_remote_copy(
-            src_ref=source.at[side, rows],
-            dst_ref=halo.at[1 - side, rows],
-            send_sem=send.at[side, at],
-            recv_sem=recv.at[1 - side, at],
-            device_id=near[axis, side],
+            src_ref=coarse.at[side, rows],
+            dst_ref=x_halo.at[1 - side, rows],
+            send_sem=x_send.at[side, at],
+            recv_sem=x_recv.at[1 - side, at],
+            device_id=core,
             device_id_type=MESH,
         )
 
-    def halo_arrival(axis, side, at):
-        halo, send, recv = (
-            (x_halo, x_send, x_recv) if axis == "sx" else (y_halo, y_send, y_recv)
-        )
+    def x_arrival(side, core, at):
         rows = pl.ds(at * chunk, chunk)
         return pltpu.make_async_remote_copy(
-            src_ref=halo.at[side, rows],
-            dst_ref=halo.at[side, rows],
-            send_sem=send.at[side, at],
-            recv_sem=recv.at[side, at],
-            device_id=near[axis, side],
+            src_ref=x_halo.at[side, rows],
+            dst_ref=x_halo.at[side, rows],
+            send_sem=x_send.at[side, at],
+            recv_sem=x_recv.at[side, at],
+            device_id=core,
             device_id_type=MESH,
         )
 
+    def y_copy(side, half, at):
+        rows = pl.ds(at * chunk, chunk)
+        return pltpu.make_async_remote_copy(
+            src_ref=across.at[side, half, rows],
+            dst_ref=y_halo.at[1 - side, half, rows],
+            send_sem=y_send.at[side, half, at],
+            recv_sem=y_recv.at[1 - side, half, at],
+            device_id=near["sy", side],
+            device_id_type=MESH,
+        )
+
+    def y_arrival(side, half, at):
+        rows = pl.ds(at * chunk, chunk)
+        return pltpu.make_async_remote_copy(
+            src_ref=y_halo.at[side, half, rows],
+            dst_ref=y_halo.at[side, half, rows],
+            send_sem=y_send.at[side, half, at],
+            recv_sem=y_recv.at[side, half, at],
+            device_id=near["sy", side],
+            device_id_type=MESH,
+        )
+
     for at in range(CHUNKS):
-        for side in range(2):
-
-            @pl.when(has["sx", side])
-            def _(side=side, at=at):
-                halo_copy("sx", side, at).start()
+
+        @pl.loop(at * (steps_chunk // 2), (at + 1) * (steps_chunk // 2))
+        def _(pair):
+            for block in range(8):
+                tile, part = block // 2, block % 2
+                half, y_half = tile // 2, tile % 2
+                both = jnp.concatenate(
+                    [
+                        turned[block, pl.ds(pair * 2, SEGMENTS, stride=steps), :],
+                        turned[block, pl.ds(pair * 2 + 1, SEGMENTS, stride=steps), :],
+                    ],
+                    axis=0,
+                )
+                lane = y_half * CELLS + part * LANES
+                coarse[half, pl.ds(pl.multiple_of(pair * 16, 16), 16), lane : lane + LANES] = (
+                    both.astype(jnp.bfloat16)
+                )
+
+        @pl.when(has_far)
+        def _(at=at):
+            x_copy(far_half, far_core, at).start()
+
+        x_copy(near_half, near_core, at).start()
 
     taps_wide[...] = jnp.zeros(taps_wide.shape, taps_wide.dtype)
     taps_wide[0:2, 0 : taps_ref.shape[1]] = taps_ref[...].astype(jnp.float32)
@@ -221,8 +242,7 @@
     def reversed_tile(tile):
         return order_ref[tile // 2, lax.rem(tile, 2)] == 1
 
-    @pl.loop(0, 4)
-    def _(tile):
+    def bumps_of(tile):
         sign = jnp.where(reversed_tile(tile), LOG2E, -LOG2E).astype(jnp.float32)
         centre = [table(centre_ref, tile, bump) for bump in range(4)]
         width = [table(width_ref, tile, bump) for bump in range(4)]
@@ -255,40 +275,54 @@
         for part in range(2):
             running[tile * 2 + part] = ends[part]
 
-    def blur(at, source, halo, band):
+    def blur_x(half, at):
         rows = slice(at * chunk, (at + 1) * chunk)
-        lines = []
-        for half in range(2):
-            for other in range(2):
-                lanes = slice(other * CELLS, (other + 1) * CELLS)
-                before = halo[0, rows, lanes] if half == 0 else source[0, rows, lanes]
-                behind = halo[1, rows, lanes] if half == 1 else source[1, rows, lanes]
-                lines.append(
-                    jnp.concatenate([before, source[half, rows, lanes], behind], axis=1)
-                )
-        return jnp.dot(
-            jnp.concatenate(lines, axis=0), band[...], preferred_element_type=jnp.float32
-        )
+        inner, outer = [], []
+        for y_half in range(2):
+            lanes = slice(y_half * CELLS, (y_half + 1) * CELLS)
+            inner.append(
+                jnp.concatenate([coarse[0, rows, lanes], coarse[1, rows, lanes]], axis=1)
+            )
+            outer.append(x_halo[half, rows, lanes])
+        inner_at = pl.multiple_of((1 - half) * CELLS, CELLS)
+        outer_at = pl.multiple_of(half * (2 * CELLS), CELLS)
+        result = jnp.dot(
+            jnp.concatenate(inner, axis=0),
+            band_x[pl.ds(inner_at, 2 * CELLS), :],
+            preferred_element_type=jnp.float32,
+        ) + jnp.dot(
+            jnp.concatenate(outer, axis=0),
+            band_x[pl.ds(outer_at, CELLS), :],
+            preferred_element_type=jnp.float32,
+        )
+        result = result.astype(jnp.bfloat16)
+        for y_half in range(2):
+            across[y_half, half, rows, :] = result[y_half * chunk : (y_half + 1) * chunk]
+        for side in range(2):
+
+            @pl.when(has["sy", side])
+            def _(side=side):
+                y_copy(side, half, at).start()
 
     for at in range(CHUNKS):
-        for side in range(2):
-
-            @pl.when(has["sx", side])
-            def _(side=side, at=at):
-                halo_arrival("sx", side, at).wait_recv()
-
-        result = blur(at, coarse, x_halo, band_x).astype(jnp.bfloat16)
-        for half in range(2):
-            for y_half in range(2):
-                place = half * 2 + y_half
-                across[
-                    y_half, at * chunk : (at + 1) * chunk, half * CELLS : (half + 1) * CELLS
-                ] = result[place * chunk : (place + 1) * chunk]
-        for side in range(2):
-
-            @pl.when(has["sy", side])
-            def _(side=side, at=at):
-                halo_copy("sy", side, at).start()
+        x_arrival(near_half, near_core, at).wait_recv()
+        blur_x(near_half, at)
+
+    @pl.loop(near_half * 2, near_half * 2 + 2)
+    def _(tile):
+        bumps_of(tile)
+
+    for at in range(CHUNKS):
+
+        @pl.when(has_far)
+        def _(at=at):
+            x_arrival(far_half, far_core, at).wait_recv()
+
+        blur_x(far_half, at)
+
+    @pl.loop(far_half * 2, far_half * 2 + 2)
+    def _(tile):
+        bumps_of(tile)
 
     sublane = lax.broadcasted_iota(jnp.int32, (SEGMENTS, LANES), 0)
     for block in range(8):
@@ -331,20 +365,36 @@
         copy.start()
     clear_in[depth] = clear[depth]
 
-    for at in range(CHUNKS):
-        for side in range(2):
-
-            @pl.when(has["sy", side])
-            def _(side=side, at=at):
-                halo_arrival("sy", side, at).wait_recv()
-
-        shade = 1.0 - jnp.tanh(blur(at, across, y_halo, band_y))
-        for y_half in range(2):
-            for half in range(2):
-                tile = half * 2 + y_half
-                place = y_half * 2 + half
+    for half in (near_half, far_half):
+        for at in range(CHUNKS):
+            for side in range(2):
+
+                @pl.when(has["sy", side])
+                def _(side=side, at=at, half=half):
+                    y_arrival(side, half, at).wait_recv()
+
+            rows = slice(at * chunk, (at + 1) * chunk)
+            before, first, second, behind = (
+                y_halo[0, half, rows, :],
+                across[0, half, rows, :],
+                across[1, half, rows, :],
+                y_halo[1, half, rows, :],
+            )
+            occlusion = jnp.dot(
+                jnp.concatenate(
+                    [
+                        jnp.concatenate([before, first, second], axis=1),
+                        jnp.concatenate([first, second, behind], axis=1),
+                    ],
+                    axis=0,
+                ),
+                band_y[...],
+                preferred_element_type=jnp.float32,
+            )
+            shade = 1.0 - jnp.tanh(occlusion)
+            for y_half in range(2):
                 for part in range(2):
-                    block = tile * 2 + part
+                    block = half * 4 + y_half * 2 + part
                     for bump in range(4):
                         total = None
                         for step in range(steps_chunk):
@@ -357,7 +407,7 @@
                                     :,
                                 ]
                                 * shade[
-                                    place * chunk + row : place * chunk + row + SEGMENTS,
+                                    y_half * chunk + row : y_half * chunk + row + SEGMENTS,
                                     part * LANES : (part + 1) * LANES,
                                 ]
                             )
@@ -420,13 +470,19 @@
             halves.append(pltpu.roll(line, SIDE, axis=1) if y_half else line)
         out_ref[channel] = jnp.where(low, halves[0], halves[1])[:, : 2 * SIDE]
 
-    for axis in ("sx", "sy"):
+    for at in range(CHUNKS):
+        x_copy(near_half, near_core, at).wait_send()
+
+        @pl.when(has_far)
+        def _(at=at):
+            x_copy(far_half, far_core, at).wait_send()
+
         for side in range(2):
-            for at in range(CHUNKS):
-
-                @pl.when(has[axis, side])
-                def _(axis=axis, side=side, at=at):
-                    halo_copy(axis, side, at).wait_send()
+
+            @pl.when(has["sy", side])
+            def _(side=side, at=at):
+                for half in range(2):
+                    y_copy(side, half, at).wait_send()
 
 
 def per_device(
@@ -447,8 +503,8 @@
             pltpu.VMEM((8, rows_z, LANES), f32),
             pltpu.VMEM((2, rows_z, 2 * CELLS), bf16),
             pltpu.VMEM((2, rows_z, 2 * CELLS), bf16),
-            pltpu.VMEM((2, rows_z, 2 * CELLS), bf16),
-            pltpu.VMEM((2, rows_z, 2 * CELLS), bf16),
+            pltpu.VMEM((2, 2, rows_z, CELLS), bf16),
+            pltpu.VMEM((2, 2, rows_z, CELLS), bf16),
             pltpu.VMEM((4, 8, rows_z, LANES), f32),
             pltpu.VMEM((3 * CELLS, CELLS), bf16),
             pltpu.VMEM((3 * CELLS, CELLS), bf16),
@@ -463,8 +519,8 @@
             pltpu.SemaphoreType.DMA((2,)),
             pltpu.SemaphoreType.DMA((2, CHUNKS)),
             pltpu.SemaphoreType.DMA((2, CHUNKS)),
-            pltpu.SemaphoreType.DMA((2, CHUNKS)),
-            pltpu.SemaphoreType.DMA((2, CHUNKS)),
+            pltpu.SemaphoreType.DMA((2, 2, CHUNKS)),
+            pltpu.SemaphoreType.DMA((2, 2, CHUNKS)),
             pltpu.SemaphoreType.DMA((n_depth - 1,)),
             pltpu.SemaphoreType.DMA((n_depth - 1,)),
             pltpu.SemaphoreType.DMA((n_depth - 1,)),

time: 28.1 us -> 28.1 us (level)
  no operation moved by 1% of the time
where the time goes in v2:
time: 28.1 us; the launch traced here: 27.9 us
  Pallas kernels  26.5 us (94%)
  local copies, waits for them, and re-layouts  1.32 us (5%)
    pallas_call x1, Pallas kernels, per_device(): pl.pallas_call(functools.partial(kernel, counts), out_shape=jax.ShapeDtyp...  26.5 us
    unnamed x1, local copies, waits for them, and re-layouts  1.32 us

profile of v2, /device:TPU:24, one launch (start us, length us, event | category | flops | bytes accessed | tf_op | source)
XLA Modules:
  0.0 27.9 jit_solution(14739029203599118429)
XLA Ops:
  0.0 26.5 %shard_map.82 = f32[4,8,32]{2,1,0:T(8,128)} custom-call(f32[32,32,256]{2,1,0:T(8,128)} %density_hbm.1, bf16[2,33]{1,0:T(2,128)(2,1)} %taps_ref.1, f32[4,8]{1,0:T(4,128)} %bitcast.9, f32[4,8]{1,0:T(4,128)} %bitcast.10, f32[3,4,8]{2,1,0:T(4,128)} %bitcast.8, f32[4,8]{1,0:T(4,128)} %bitcast.11, s32[2,2,2]{2,1,0:T(2,128)} %brick_ref.1, s32[2,2]{1,0:T(2,128)} %order_ref.1), custom_call_target="tpu_custom_call" | custom-call | tf_op jit(solution)/shard_map/pallas_call | solution.py:496
  26.5 1.3 %copy.11 = f32[4,1,1,8,32]{4,3,2,1,0:T(8,128)} copy(f32[4,1,1,8,32]{4,3,2,1,0:T(8,128)} %bitcast.7) | data formatting | bytes 8192

commit v3 on v2

--- a/solution.py
+++ b/solution.py
@@ -49,6 +49,14 @@
 def kernel(
     counts,
     density_hbm,
+    taps_hbm,
+    centre_hbm,
+    width_hbm,
+    color_hbm,
+    opacity_hbm,
+    brick_hbm,
+    order_hbm,
+    out_ref,
     taps_ref,
     centre_ref,
     width_ref,
@@ -56,7 +64,7 @@
     opacity_ref,
     brick_ref,
     order_ref,
-    out_ref,
+    table_sem,
     density,
     turned,
     coarse,
@@ -134,6 +142,21 @@
             device_id_type=MESH,
         )
 
+    tables = (
+        (taps_hbm, taps_ref),
+        (centre_hbm, centre_ref),
+        (width_hbm, width_ref),
+        (color_hbm, color_ref),
+        (opacity_hbm, opacity_ref),
+        (brick_hbm, brick_ref),
+        (order_hbm, order_ref),
+    )
+    table_loads = []
+    for at, (source, target) in enumerate(tables):
+        copy = pltpu.make_async_copy(source, target, table_sem.at[at])
+        copy.start()
+        table_loads.append(copy)
+
     for axis, halo in (("sx", x_halo), ("sy", y_halo)):
         for side in range(2):
 
@@ -224,6 +247,8 @@
 
         x_copy(near_half, near_core, at).start()
 
+    for copy in table_loads:
+        copy.wait()
     taps_wide[...] = jnp.zeros(taps_wide.shape, taps_wide.dtype)
     taps_wide[0:2, 0 : taps_ref.shape[1]] = taps_ref[...].astype(jnp.float32)
     band_x[...] = band_tiles(taps_wide[0:1, :], True, 1.0)
@@ -491,14 +516,21 @@
     rows_x, rows_y, rows_z = density.shape
     n_depth = counts[0]
     f32, bf16 = jnp.float32, jnp.bfloat16
-    smem = pl.BlockSpec(memory_space=pltpu.SMEM)
     vmem = pl.BlockSpec(memory_space=pltpu.VMEM)
     picture = pl.pallas_call(
         functools.partial(kernel, counts),
         out_shape=jax.ShapeDtypeStruct((4, rows_x // n_depth, rows_y), f32),
-        in_specs=[pl.BlockSpec(memory_space=pl.ANY), vmem] + [smem] * 6,
+        in_specs=[pl.BlockSpec(memory_space=pl.ANY)] * 8,
         out_specs=vmem,
         scratch_shapes=[
+            pltpu.VMEM(kernel_taps.shape, bf16),
+            pltpu.SMEM(tf_centre.shape[::-1], f32),
+            pltpu.SMEM(tf_width.shape[::-1], f32),
+            pltpu.SMEM(tf_color.shape[::-1], f32),
+            pltpu.SMEM(tf_opacity.shape[::-1], f32),
+            pltpu.SMEM(brick_tf.shape, jnp.int32),
+            pltpu.SMEM(view_order.shape, jnp.int32),
+            pltpu.SemaphoreType.DMA((7,)),
             pltpu.VMEM((rows_x, rows_y, rows_z), f32),
             pltpu.VMEM((8, rows_z, LANES), f32),
             pltpu.VMEM((2, rows_z, 2 * CELLS), bf16),

time: 28.1 us -> 27 us (0.961)
  Pallas kernels: 26.5 us -> 25.5 us
    pallas_call x1, Pallas kernels: 26.5 us -> 25.5 us  [per_device(): pl.pallas_call(functools.partial(kernel, counts), out_shape=jax.ShapeDtyp...]
where the time goes in v3:
time: 27 us; the launch traced here: 26.9 us
  Pallas kernels  25.5 us (94%)
  local copies, waits for them, and re-layouts  1.32 us (5%)
    pallas_call x1, Pallas kernels, per_device(): pl.pallas_call(functools.partial(kernel, counts), out_shape=jax.ShapeDtyp...  25.5 us
    unnamed x1, local copies, waits for them, and re-layouts  1.32 us

profile of v3, /device:TPU:24, one launch (start us, length us, event | category | flops | bytes accessed | tf_op | source)
XLA Modules:
  0.0 26.9 jit_solution(11096801032191705402)
XLA Ops:
  0.0 25.5 %shard_map.82 = f32[4,8,32]{2,1,0:T(8,128)} custom-call(f32[32,32,256]{2,1,0:T(8,128)} %density_hbm.1, bf16[2,33]{1,0:T(2,128)(2,1)} %taps_hbm.1, f32[4,8]{1,0:T(4,128)} %bitcast.9, f32[4,8]{1,0:T(4,128)} %bitcast.10, f32[3,4,8]{2,1,0:T(4,128)} %bitcast.8, f32[4,8]{1,0:T(4,128)} %bitcast.11, s32[2,2,2]{2,1,0:T(2,128)} %brick_hbm.1, s32[2,2]{1,0:T(2,128)} %order_hbm.1), custom_call_target="tpu_custom_call" | custom-call | tf_op jit(solution)/shard_map/pallas_call | solution.py:520
  25.5 1.3 %copy.11 = f32[4,1,1,8,32]{4,3,2,1,0:T(8,128)} copy(f32[4,1,1,8,32]{4,3,2,1,0:T(8,128)} %bitcast.7) | data formatting | bytes 8192

commit v4 on v3

--- a/solution.py
+++ b/solution.py
@@ -9,7 +9,7 @@
 
 MESH = pl.DeviceIdType.MESH
 LOG2E = 1.4426950408889634
-CHUNKS = 4
+CHUNKS = 2
 SIDE = 16
 CELLS = SIDE * SIDE
 LANES = 128
@@ -56,6 +56,7 @@
     opacity_hbm,
     brick_hbm,
     order_hbm,
+    out_hbm,
     out_ref,
     taps_ref,
     centre_ref,
@@ -65,6 +66,7 @@
     brick_ref,
     order_ref,
     table_sem,
+    out_sem,
     density,
     turned,
     coarse,
@@ -117,6 +119,21 @@
     near_core = {"sx": sx + 2 * near_half - 1}
     far_core = {"sx": jnp.clip(sx + 2 * far_half - 1, 0, n_sx - 1)}
 
+    barrier = pltpu.get_barrier_semaphore()
+    for key, there in has.items():
+
+        @pl.when(there)
+        def _(key=key):
+            pl.semaphore_signal(barrier, inc=1, device_id=near[key], device_id_type=MESH)
+
+    for step in range(1, n_depth):
+        pl.semaphore_signal(
+            barrier,
+            inc=1,
+            device_id={"depth": lax.rem(depth + step, n_depth)},
+            device_id_type=MESH,
+        )
+
     loads = []
     for half in range(2):
         copy = pltpu.make_async_copy(
@@ -126,21 +143,6 @@
         )
         copy.start()
         loads.append(copy)
-
-    barrier = pltpu.get_barrier_semaphore()
-    for key, there in has.items():
-
-        @pl.when(there)
-        def _(key=key):
-            pl.semaphore_signal(barrier, inc=1, device_id=near[key], device_id_type=MESH)
-
-    for step in range(1, n_depth):
-        pl.semaphore_signal(
-            barrier,
-            inc=1,
-            device_id={"depth": lax.rem(depth + step, n_depth)},
-            device_id_type=MESH,
-        )
 
     tables = (
         (taps_hbm, taps_ref),
@@ -495,6 +497,8 @@
             halves.append(pltpu.roll(line, SIDE, axis=1) if y_half else line)
         out_ref[channel] = jnp.where(low, halves[0], halves[1])[:, : 2 * SIDE]
 
+    result_copy = pltpu.make_async_copy(out_ref, out_hbm, out_sem)
+    result_copy.start()
     for at in range(CHUNKS):
         x_copy(near_half, near_core, at).wait_send()
 
@@ -508,6 +512,8 @@
             def _(side=side, at=at):
                 for half in range(2):
                     y_copy(side, half, at).wait_send()
+
+    result_copy.wait()
 
 
 def per_device(
@@ -516,13 +522,13 @@
     rows_x, rows_y, rows_z = density.shape
     n_depth = counts[0]
     f32, bf16 = jnp.float32, jnp.bfloat16
-    vmem = pl.BlockSpec(memory_space=pltpu.VMEM)
     picture = pl.pallas_call(
         functools.partial(kernel, counts),
         out_shape=jax.ShapeDtypeStruct((4, rows_x // n_depth, rows_y), f32),
         in_specs=[pl.BlockSpec(memory_space=pl.ANY)] * 8,
-        out_specs=vmem,
+        out_specs=pl.BlockSpec(memory_space=pl.ANY),
         scratch_shapes=[
+            pltpu.VMEM((4, rows_x // n_depth, rows_y), f32),
             pltpu.VMEM(kernel_taps.shape, bf16),
             pltpu.SMEM(tf_centre.shape[::-1], f32),
             pltpu.SMEM(tf_width.shape[::-1], f32),
@@ -531,6 +537,7 @@
             pltpu.SMEM(brick_tf.shape, jnp.int32),
             pltpu.SMEM(view_order.shape, jnp.int32),
             pltpu.SemaphoreType.DMA((7,)),
+            pltpu.SemaphoreType.DMA,
             pltpu.VMEM((rows_x, rows_y, rows_z), f32),
             pltpu.VMEM((8, rows_z, LANES), f32),
             pltpu.VMEM((2, rows_z, 2 * CELLS), bf16),

time: 27 us -> 26.8 us (level)
    pallas_call x1, Pallas kernels: 25.5 us -> 25.3 us  [per_device(): pl.pallas_call(functools.partial(kernel, counts), out_shape=jax.ShapeDtyp...]
where the time goes in v4:
time: 26.8 us; the launch traced here: 26.6 us
  Pallas kernels  25.3 us (94%)
  local copies, waits for them, and re-layouts  1.32 us (5%)
    pallas_call x1, Pallas kernels, per_device(): pl.pallas_call(functools.partial(kernel, counts), out_shape=jax.ShapeDtyp...  25.3 us
    unnamed x1, local copies, waits for them, and re-layouts  1.32 us

profile of v4, /device:TPU:24, one launch (start us, length us, event | category | flops | bytes accessed | tf_op | source)
XLA Modules:
  0.0 26.6 jit_solution(4622038486737737234)
XLA Ops:
  0.0 25.3 %shard_map.82 = f32[4,8,32]{2,1,0:T(8,128)} custom-call(f32[32,32,256]{2,1,0:T(8,128)} %density_hbm.1, bf16[2,33]{1,0:T(2,128)(2,1)} %taps_hbm.1, f32[4,8]{1,0:T(4,128)} %bitcast.9, f32[4,8]{1,0:T(4,128)} %bitcast.10, f32[3,4,8]{2,1,0:T(4,128)} %bitcast.8, f32[4,8]{1,0:T(4,128)} %bitcast.11, s32[2,2,2]{2,1,0:T(2,128)} %brick_hbm.1, s32[2,2]{1,0:T(2,128)} %order_hbm.1), custom_call_target="tpu_custom_call" | custom-call | tf_op jit(solution)/shard_map/pallas_call | solution.py:525
  25.3 1.3 %copy.11 = f32[4,1,1,8,32]{4,3,2,1,0:T(8,128)} copy(f32[4,1,1,8,32]{4,3,2,1,0:T(8,128)} %bitcast.7) | data formatting | bytes 8192
